TPU v7x, 32 devices: a whole 2x2x4 slice. The times are simulated.
32 devices in a mesh: rep: 4 (over y, core), tp: 8 (over z, x).
Axes of the slice: x: 2, y: 2, z: 4, core: 2. Of those that a mesh axis runs over, the one named last changes fastest.
Arguments:
- tokens: bfloat16 [2560, 5120], P(('rep', 'tp')), parts along dimension 0
- weights: bfloat16 [3, 5120, 4096], P(None, None, 'tp')
- modulation: float32 [2, 36, 5120], P(None, 'rep'), parts along dimension 1, may hold values from -3 to 3
- qk_gain: float32 [2, 4096], P(None, 'tp'), may hold values from 0.25 to 1.75
- segment_ids: int32 [2560], P('rep'), parts along dimension 0, may hold values from 0 to 9, as said below
- positions: int32 [3, 2560], P(None, 'rep'), parts along dimension 1, may hold values from 0 to 15, as said below
- page_table: int32 [160], P('rep'), parts along dimension 0, may hold values from 0 to 79, as said below
- kv_cache: bfloat16 [2, 32, 320, 16, 128], P(None, 'tp', 'rep'), parts along dimension 2, may hold values from -6 to 6
Outputs:
- attended: bfloat16 [2560, 4096], P(('rep', 'tp')), parts along dimension 0
- new_cache: bfloat16 [2, 32, 320, 16, 128], P(None, 'tp', 'rep'), parts along dimension 2
There are 4 independent parts, one for each index of `rep`. A program takes and returns all parts, laid end to end along the dimension named above; an argument that names none is the same for every part. Nothing has to cross between parts.
Inputs may be any that keep to these rules, and one draw needn't show every extreme that they name: `segment_ids`: never falling; 0 on the first 512 tokens (the long clip); then clips 1 to 8 in order, each of 8 to 16 tokens, at least one of exactly 16; the remaining tokens are padding with id 9. `positions`: each token's frame, height and width index on its clip's grid; 0 on padding tokens. `page_table`: distinct pages.
All inputs are finite; a program needn't handle non-finite values.
Results may differ from a plain program's by a relative error of at most 0.0047.
Values may be sent and summed in bfloat16 or wider, within the bound.
No kernel may reach another device: no remote copies, remote signals or barrier semaphores. Data moves between devices by JAX's collectives and lax.ppermute only.
A program may use at most 128 MiB of HBM per device.

v0:
```python
import math
import jax
import jax.numpy as jnp
import numpy as np
from jax import lax
from jax.sharding import PartitionSpec as P

HEAD = 128
HEADS = 32
PAGE = 16
epsilon = 1e-06
masked_score = -1e30


def rotary_tables(positions, head_size):
    height_dims = 2 * (head_size // 6)
    frame_dims = head_size - 2 * height_dims
    frame_freq = 1.0 / 10000.0 ** (np.arange(0, frame_dims, 2) / frame_dims)
    height_freq = 1.0 / 10000.0 ** (np.arange(0, height_dims, 2) / height_dims)
    zero_frame = np.zeros(frame_dims // 2)
    zero_height = np.zeros(height_dims // 2)
    table_frame = np.concatenate([frame_freq, zero_height, zero_height])
    table_height = np.concatenate([zero_frame, height_freq, zero_height])
    table_width = np.concatenate([zero_frame, zero_height, height_freq])
    coords = positions.astype(jnp.float32)
    angles = coords[0][:, None] * jnp.asarray(table_frame, jnp.float32)[None, :]
    angles = angles + coords[1][:, None] * jnp.asarray(table_height, jnp.float32)[None, :]
    angles = angles + coords[2][:, None] * jnp.asarray(table_width, jnp.float32)[None, :]
    return (jnp.cos(angles), jnp.sin(angles))


def rotary_apply(channels, cosine, sine_table):
    first = channels[..., 0::2]
    second = channels[..., 1::2]
    cos_rows = cosine[:, None, :]
    sin_rows = sine_table[:, None, :]
    turned = jnp.stack(
        [first * cos_rows - second * sin_rows, first * sin_rows + second * cos_rows], axis=-1
    )
    return turned.reshape(channels.shape)


def layer_norm_mod(rows, seg_rows, modulation):
    floats = rows.astype(jnp.float32)
    center = floats - jnp.mean(floats, axis=1, keepdims=True)
    spread = jnp.mean(center * center, axis=1, keepdims=True)
    normed = center * lax.rsqrt(spread + epsilon)
    onehot = (
        seg_rows[:, None] == jnp.arange(modulation.shape[1], dtype=jnp.int32)[None, :]
    ).astype(jnp.float32)
    shifts = jnp.dot(onehot, modulation[0], precision=lax.Precision.HIGHEST)
    scales = jnp.dot(onehot, modulation[1], precision=lax.Precision.HIGHEST)
    return (normed * (1.0 + scales) + shifts).astype(jnp.bfloat16)


def attend_block(q_block, key_all, value_all, seg_query, seg_keys, clip_count):
    scaling = float(q_block.shape[2]) ** (-0.5)
    scores = (
        jnp.einsum("qhd,khd->hqk", q_block, key_all, preferred_element_type=jnp.float32) * scaling
    )
    query_live = seg_query < clip_count
    allowed = (seg_query[:, None] == seg_keys[None, :]) & query_live[:, None]
    scores = jnp.where(allowed[None], scores, masked_score)
    row_top = jnp.max(scores, axis=2, keepdims=True)
    exponent = jnp.exp(scores - row_top)
    row_total = jnp.sum(exponent, axis=2)
    probabilities = exponent.astype(jnp.bfloat16)
    result = jnp.einsum(
        "hqk,khd->qhd", probabilities, value_all, preferred_element_type=jnp.float32
    )
    result = result / row_total.T[:, :, None]
    return jnp.where(query_live[:, None, None], result, 0.0).astype(jnp.bfloat16)


def attend_range(q_rot, k_rot, v_low, segment_ids, clip_count, row_low, row_high):
    block_rows = math.gcd(row_high - row_low, 512)
    results = []
    for row_start in range(row_low, row_high, block_rows):
        q_block = q_rot[row_start : row_start + block_rows]
        seg_query = segment_ids[row_start : row_start + block_rows]
        results.append(attend_block(q_block, k_rot, v_low, seg_query, segment_ids, clip_count))
    return jnp.concatenate(results, axis=0)


def body(tokens, weights, modulation, qk_gain, segment_ids, positions, page_table, kv_cache):
    tok_rows = tokens.shape[0]
    head_here = weights.shape[2] // HEAD
    self_rank = lax.axis_index("tp")
    own_seg = lax.dynamic_slice_in_dim(segment_ids, self_rank * tok_rows, tok_rows)
    x_mod = layer_norm_mod(tokens, own_seg, modulation)
    projected = jnp.einsum(
        "td,cdh->tch",
        lax.all_gather(x_mod, "tp", axis=0, tiled=True),
        weights,
        preferred_element_type=jnp.float32,
    )
    total_rows = projected.shape[0]
    queries = projected[:, 0]
    key_rows = projected[:, 1]
    values = projected[:, 2]
    q_part = jnp.sum(queries * queries, axis=1)
    k_part = jnp.sum(key_rows * key_rows, axis=1)
    q_total, k_total = lax.psum((q_part, k_part), "tp")
    channels = HEADS * HEAD
    q_mean = q_total / channels
    k_mean = k_total / channels
    cosine, sine_table = rotary_tables(positions, HEAD)
    q_norm = queries * lax.rsqrt(q_mean + epsilon)[:, None] * qk_gain[0][None, :]
    k_norm = key_rows * lax.rsqrt(k_mean + epsilon)[:, None] * qk_gain[1][None, :]
    q_rot = rotary_apply(q_norm.reshape(total_rows, head_here, HEAD), cosine, sine_table).astype(
        jnp.bfloat16
    )
    k_rot = rotary_apply(k_norm.reshape(total_rows, head_here, HEAD), cosine, sine_table).astype(
        jnp.bfloat16
    )
    v_low = values.astype(jnp.bfloat16).reshape(total_rows, head_here, HEAD)
    clip_count = modulation.shape[1]
    heads_out = attend_range(q_rot, k_rot, v_low, segment_ids, clip_count, 0, total_rows)
    local_heads = heads_out.reshape(total_rows, head_here * HEAD)
    attended = lax.all_to_all(local_heads, "tp", split_axis=0, concat_axis=1, tiled=True)
    page_count = total_rows // PAGE
    stacked = jnp.stack([k_rot, v_low]).reshape(2, page_count, PAGE, head_here, HEAD)
    paged = stacked.transpose(0, 3, 1, 2, 4)
    new_cache = kv_cache.at[:, :, page_table].set(paged)
    return (attended, new_cache)


def solution(mesh):
    return jax.shard_map(
        body,
        mesh=mesh,
        in_specs=(
            P(("rep", "tp"), None),
            P(None, None, "tp"),
            P(None, "rep", None),
            P(None, "tp"),
            P("rep"),
            P(None, "rep"),
            P("rep"),
            P(None, "tp", "rep", None, None),
        ),
        out_specs=(P(("rep", "tp"), None), P(None, "tp", "rep", None, None)),
        check_vma=False,
    )
```

profile of v0, /device:TPU:0, one launch (start us, length us, event | category | flops | bytes accessed | tf_op | source)
XLA Modules:
  0.0 209.8 jit_solution(9179816247852573089)
XLA Ops:
  7.2 1.1 copy-done
  9.3 1.0 fusion.2
  10.4 1.7 fusion.3
  12.3 1.4 fusion.55
  13.7 1.0 compare_and_fusion
  14.7 102.2 %all-gather.2.cloned.1.call-done = bf16[640,5120]{1,0:T(8,128)(2,1)} async-done(((bf16[80,5120]{1,0:T(8,128)(2,1)}), bf16[640,5120]{1,0:T(8,128)(2,1)}) %all-gather.2.cloned.1.call-update) | async-done | bytes 6553616 | tf_op jit(solution)/shard_map/all_gather | solution.py:93
  116.9 16.9 %fusion = f32[640,3,512]{0,2,1:T(8,128)S(1)} fusion(bf16[3,5120,512]{2,1,0:T(8,128)(2,1)} %param.12, bf16[640,5120]{1,0:T(8,128)(2,1)} %all-gather.2.cloned.1.call-done), kind=kOutput, calls=%fused_computation.1 | convolution fusion | flops 10066329600 | bytes 26214400 | tf_op jit(solution)/shard_map/td,cdh->tch/dot_general | solution.py:91
  134.3 19.0 %all-reduce = (f32[640]{0:T(1024)S(1)}, f32[640]{0:T(1024)S(1)}) all-reduce(f32[640]{0:T(1024)S(1)} %get-tuple-element.3, f32[640]{0:T(1024)S(1)} %get-tuple-element.2), channel_id=1, replica_groups=mesh['rep'=4,'tp'=8] {'tp'}, use_global_device_ids=true, to_apply=%region_3.0 | all-reduce | flops 1280 | bytes 10240 | tf_op jit(solution)/shard_map/psum | solution.py:103
  153.3 1.2 multiply_multiply_fusion.1
  154.5 3.4 %slice.97 = f32[640,4,64]{0,2,1:T(8,128)} slice(f32[640,4,128]{0,2,1:T(8,128)} %multiply_multiply_fusion.1), slice={[0:640:1], [0:4:1], [1:128:2]} | slice | bytes 1310720 | tf_op jit(solution)/shard_map/slice | solution.py:34
  158.0 1.5 slice.93
  160.3 1.5 fusion.53
  161.8 0.9 pad_maximum_fusion
  162.7 0.8 copy.88
  164.5 1.4 maximum_convert_fusion
  165.9 0.8 copy.90
  177.0 1.1 all_to_all.14
  178.1 4.2 %all-to-all-start = ((bf16[8,80,512]{2,1,0:T(8,128)(2,1)}), bf16[8,80,512]{2,1,0:T(8,128)(2,1)}, u32[]{:S(2)}, u32[]{:S(2)}) async-start(bf16[8,80,512]{2,1,0:T(8,128)(2,1)} %all_to_all.14), calls=%async_computation | async-start | bytes 1310720 | tf_op jit(solution)/shard_map/all_to_all | solution.py:120
  182.6 5.0 %convert_element_type.94 = bf16[1,40,16,4,128]{2,1,4,3,0:T(8,128)(2,1)} reshape(bf16[640,4,64,2]{0,3,2,1:T(2,128)(2,1)S(1)} %maximum_convert_fusion) | data formatting | bytes 1310720 | tf_op jit(solution)/shard_map/convert_element_type | solution.py:113
  187.9 4.6 %copy.113 = bf16[1,40,16,4,128]{4,2,3,1,0:T(8,128)(2,1)S(1)} copy(bf16[1,40,16,4,128]{2,1,4,3,0:T(8,128)(2,1)} %convert_element_type.94) | data formatting | bytes 1310720 | tf_op jit(solution)/shard_map/convert_element_type | solution.py:113
  192.6 1.3 copy.115
  193.9 0.9 copy-done.2
  194.8 5.6 %scatter_fusion = bf16[2,4,80,16,128]{4,3,2,1,0:T(8,128)(2,1)S(1)} fusion(bf16[2,4,80,16,128]{4,3,2,1,0:T(8,128)(2,1)S(1)} %copy-done.2, s32[40]{0:T(128)S(1)} %compare_select_fusion, bf16[40,2,4,16,128]{4,3,2,1,0:T(8,128)(2,1)} %copy.115), kind=kCustom, calls=%fused_computation | custom fusion | bytes 3932320 | tf_op jit(solution)/shard_map/scatter | solution.py:124
  200.4 2.5 %copy.129 = bf16[8,10,8,512]{3,2,0,1:T(8,128)(2,1)} copy(bf16[8,10,8,512]{3,2,1,0:T(8,128)(2,1)} %bitcast.29) | data formatting | bytes 1310720 | tf_op jit(solution)/shard_map/all_to_all | solution.py:120
  (103 shorter events, 14.0 us)
Async XLA Ops:
  7.2 1.1 copy-start
  7.2 109.7 %all-gather.2.cloned.1.call-start = ((), (), s32[]{:S(2)}) async-start(), calls=%async_computation.1 | async-start | bytes 7372800 | tf_op jit(solution)/shard_map/all_gather | solution.py:93
  7.2 1.7 copy-start.10
  7.2 2.0 copy-start.15
  10.3 1.8 copy-start.16
  10.3 1.9 copy-start.17
  10.3 2.0 copy-start.24
  10.4 1.9 copy-start.25
  10.4 1.9 copy-start.26
  12.3 121.6 %copy-start.18 = (pred[128]{0:T(512)(128)(4,1)}, pred[128]{0:T(512)(128)(4,1)S(1)}, u32[]{:S(2)}) copy-start(pred[128]{0:T(512)(128)(4,1)S(1)} %get-tuple-element.32) | copy-start | bytes 388
  12.3 121.6 %copy-start.20 = (pred[128]{0:T(512)(128)(4,1)}, pred[128]{0:T(512)(128)(4,1)S(1)}, u32[]{:S(2)}) copy-start(pred[128]{0:T(512)(128)(4,1)S(1)} %get-tuple-element.31) | copy-start | bytes 388
  12.3 121.6 %copy-start.22 = (pred[128]{0:T(512)(128)(4,1)}, pred[128]{0:T(512)(128)(4,1)S(1)}, u32[]{:S(2)}) copy-start(pred[128]{0:T(512)(128)(4,1)S(1)} %get-tuple-element.30) | copy-start | bytes 388
  154.5 3.5 %copy-start.3 = (f32[640,4,128]{0,2,1:T(8,128)S(1)}, f32[640,4,128]{0,2,1:T(8,128)}, u32[]{:S(2)}) copy-start(f32[640,4,128]{0,2,1:T(8,128)} %multiply_multiply_fusion.1) | copy-start | bytes 3932164
  161.8 1.7 copy-start.4
  165.9 1.7 copy-start.9
  165.9 1.9 copy-start.8
  165.9 2.0 copy-start.7
  166.8 1.3 copy-start.6
  166.8 1.4 copy-start.5
  166.8 1.4 copy-start.14
  177.0 5.3 %copy-start.27 = (s32[40]{0:T(128)S(1)}, s32[40]{0:T(128)}, u32[]{:S(2)}) copy-start(s32[40]{0:T(128)} %param.17) | copy-start | bytes 484
  178.1 22.4 %all-to-all-start = ((bf16[8,80,512]{2,1,0:T(8,128)(2,1)}), bf16[8,80,512]{2,1,0:T(8,128)(2,1)}, u32[]{:S(2)}, u32[]{:S(2)}) async-start(bf16[8,80,512]{2,1,0:T(8,128)(2,1)} %all_to_all.14), calls=%async_computation | async-start | bytes 1310720 | tf_op jit(solution)/shard_map/all_to_all | solution.py:120
  192.6 2.2 %copy-start.2 = (bf16[2,4,80,16,128]{4,3,2,1,0:T(8,128)(2,1)S(1)}, bf16[2,4,80,16,128]{4,3,2,1,0:T(8,128)(2,1)}, u32[]{:S(2)}) copy-start(bf16[2,4,80,16,128]{4,3,2,1,0:T(8,128)(2,1)} %param.18) | copy-start | bytes 7864324
  200.4 2.5 %copy-start.1 = (bf16[2,4,80,16,128]{4,3,2,1,0:T(8,128)(2,1)}, bf16[2,4,80,16,128]{4,3,2,1,0:T(8,128)(2,1)S(1)}, u32[]{:S(2)}) copy-start(bf16[2,4,80,16,128]{4,3,2,1,0:T(8,128)(2,1)S(1)} %scatter_fusion) | copy-start | bytes 7864324
  (6 other events, 5.4 us)
Sparse Core Ops, SparseCore 0:
  12.3 104.5 all-gather.1
where the time goes:
time: 210 us
  waiting for transfers between devices  102 us (49%)
  local copies, waits for them, and re-layouts  34.4 us (16%)
  matrix products  24.6 us (12%)
  blocking collectives  19 us (9%)
  between operations  14.7 us (7%)
  other arithmetic  10.6 us (5%)
  starting transfers between devices  4.25 us (2%)
    all_gather x1, waiting for transfers between devices, body(): lax.all_gather(x_mod, 'tp', axis=0, tiled=True)  102 us
    psum x1, blocking collectives, body(): q_total, k_total = lax.psum((q_part, k_part), 'tp')  19 us
    dot_general x1, matrix products, body(): jnp.einsum('td,cdh->tch', lax.all_gather(x_mod, 'tp', axis=0, tiled=True)...  16.9 us
    convert_element_type x4, local copies, waits for them, and re-layouts, body(): rotary_apply(k_norm.reshape(total_rows, head_here, HEAD), cosine, sine_ta...  11.3 us
    scatter x1, local copies, waits for them, and re-layouts, body(): new_cache = kv_cache.at[:, :, page_table].set(paged)  5.59 us
    all_to_all x1, starting transfers between devices, body(): lax.all_to_all(local_heads, 'tp', split_axis=0, concat_axis=1, tiled=True)  4.21 us
  transfers between devices with their start and end apart: 2, of which 1 were waited for; matrix products, arithmetic and copies ran while one was open for 9% of the time, Pallas kernels for 0%

commit v1 on v0

--- a/solution.py
+++ b/solution.py
@@ -10,6 +10,27 @@
 PAGE = 16
 epsilon = 1e-06
 masked_score = -1e30
+
+
+def in_order(tiles, dim):
+    dims = list(tiles.shape[1:])
+    dims[dim] *= tiles.shape[0]
+    return jnp.moveaxis(tiles, 0, dim).reshape(dims)
+
+
+def doubled(x, axis):
+    size, mine = (lax.axis_size(axis), lax.axis_index(axis))
+    parts, bit = (x[None], 1)
+    while bit < size:
+        other = lax.ppermute(parts, axis, [(i, i ^ bit) for i in range(size)])
+        low = mine & bit == 0
+        parts = jnp.concatenate([jnp.where(low, parts, other), jnp.where(low, other, parts)])
+        bit *= 2
+    return parts
+
+
+def doubled_up(x, axis, dim):
+    return in_order(doubled(x, axis), dim)
 
 
 def rotary_tables(positions, head_size):
@@ -89,10 +110,7 @@
     own_seg = lax.dynamic_slice_in_dim(segment_ids, self_rank * tok_rows, tok_rows)
     x_mod = layer_norm_mod(tokens, own_seg, modulation)
     projected = jnp.einsum(
-        "td,cdh->tch",
-        lax.all_gather(x_mod, "tp", axis=0, tiled=True),
-        weights,
-        preferred_element_type=jnp.float32,
+        "td,cdh->tch", doubled_up(x_mod, "tp", 0), weights, preferred_element_type=jnp.float32
     )
     total_rows = projected.shape[0]
     queries = projected[:, 0]

time: 210 us -> 309 us (1.47)
  waiting for transfers between devices: 102 us -> 191 us
  between operations: 14.7 us -> 1.2 us
  other arithmetic: 10.6 us -> 20.4 us
  starting transfers between devices: 4.25 us -> 11.6 us
  local copies, waits for them, and re-layouts: 34.4 us -> 38.6 us
    ppermute x0 -> x3, waiting for transfers between devices: none -> 191 us  [doubled(): other = lax.ppermute(parts, axis, [(i, i ^ bit) for i in range(size)])]
    all_gather x1 -> x0, waiting for transfers between devices: 102 us -> none  [body(): lax.all_gather(x_mod, 'tp', axis=0, tiled=True)]
    ppermute x0 -> x3, starting transfers between devices: none -> 7.42 us  [doubled(): other = lax.ppermute(parts, axis, [(i, i ^ bit) for i in range(size)])]
    concatenate x0 -> x3, other arithmetic: none -> 5.42 us  [doubled(): jnp.concatenate([jnp.where(low, parts, other), jnp.where(low, other, part...]
    select_n x0 -> x3, other arithmetic: none -> 4.37 us  [doubled(): jnp.where(low, parts, other)]
    slice x2, local copies, waits for them, and re-layouts: 1.83 us -> 5 us  [rotary_apply(): first = channels[..., 0::2]]
  transfers between devices with their start and end apart: 2 -> 4, of which waited for: 1 -> 3; matrix products, arithmetic and copies ran while one was open for 9% -> 6% of each run, Pallas kernels for 0% -> 0%
where the time goes in v1:
time: 309 us; the launch traced here: 308 us
  waiting for transfers between devices  191 us (62%)
  local copies, waits for them, and re-layouts  38.6 us (12%)
  matrix products  23.7 us (8%)
  blocking collectives  21.5 us (7%)
  other arithmetic  20.4 us (7%)
  starting transfers between devices  11.6 us (4%)
    ppermute x3, waiting for transfers between devices, doubled(): other = lax.ppermute(parts, axis, [(i, i ^ bit) for i in range(size)])  191 us
    psum x1, blocking collectives, body(): q_total, k_total = lax.psum((q_part, k_part), 'tp')  21.5 us
    dot_general x1, matrix products, body(): jnp.einsum('td,cdh->tch', doubled_up(x_mod, 'tp', 0), weights, preferred_...  16.9 us
    convert_element_type x4, local copies, waits for them, and re-layouts, body(): rotary_apply(k_norm.reshape(total_rows, head_here, HEAD), cosine, sine_ta...  11.3 us
    ppermute x3, starting transfers between devices, doubled(): other = lax.ppermute(parts, axis, [(i, i ^ bit) for i in range(size)])  7.42 us
  transfers between devices with their start and end apart: 4, of which 3 were waited for; matrix products, arithmetic and copies ran while one was open for 6% of the time, Pallas kernels for 0%

profile of v1, /device:TPU:0, one launch (start us, length us, event | category | flops | bytes accessed | tf_op | source)
XLA Modules:
  0.0 308.1 jit_solution(4577884173509545929)
XLA Ops:
  4.5 3.0 collective-permute-start
  7.5 18.2 %collective-permute-done = bf16[1,80,5120]{2,1,0:T(8,128)(2,1)S(1)} collective-permute-done((bf16[1,80,5120]{2,1,0:T(8,128)(2,1)S(1)}, bf16[1,80,5120]{2,1,0:T(8,128)(2,1)S(1)}, u32[]{:S(2)}, u32[]{:S(2)}) %collective-permute-start) | collective-permute-done | bytes 819232 | tf_op jit(solution)/shard_map/ppermute | solution.py:25
  27.0 1.8 collective-permute-start.1
  28.9 35.2 %collective-permute-done.1 = bf16[2,80,5120]{2,1,0:T(8,128)(2,1)} collective-permute-done((bf16[2,80,5120]{2,1,0:T(8,128)(2,1)S(1)}, bf16[2,80,5120]{2,1,0:T(8,128)(2,1)}, u32[]{:S(2)}, u32[]{:S(2)}) %collective-permute-start.1) | collective-permute-done | bytes 1638432 | tf_op jit(solution)/shard_map/ppermute | solution.py:25
  64.1 2.1 broadcast_select_fusion.3
  66.3 2.0 pad_maximum_fusion.1
  68.2 2.6 collective-permute-start.2
  73.3 137.6 %collective-permute-done.2 = bf16[4,80,5120]{2,1,0:T(8,128)(2,1)} collective-permute-done((bf16[4,80,5120]{2,1,0:T(8,128)(2,1)}, bf16[4,80,5120]{2,1,0:T(8,128)(2,1)}, u32[]{:S(2)}, u32[]{:S(2)}) %collective-permute-start.2) | collective-permute-done | bytes 3276832 | tf_op jit(solution)/shard_map/ppermute | solution.py:25
  210.9 2.2 broadcast_select_fusion.1
  213.1 3.3 %pad_maximum_fusion = bf16[8,80,5120]{2,1,0:T(8,128)(2,1)} fusion(bf16[4,80,5120]{2,1,0:T(8,128)(2,1)S(1)} %get-tuple-element.10, bf16[4,80,5120]{2,1,0:T(8,128)(2,1)S(1)} %get-tuple-element.9), kind=kLoop, calls=%fused_computation.1 | loop fusion | flops 3276800 | bytes 13107200 | tf_op jit(solution)/shard_map/concatenate | solution.py:27
  216.4 16.9 %fusion.69 = f32[640,3,512]{0,2,1:T(8,128)S(1)} fusion(bf16[640,5120,1]{1,0,2:T(8,128)(2,1)} %bitcast.111, bf16[3,5120,512]{2,1,0:T(8,128)(2,1)} %param.12), kind=kOutput, calls=%fused_computation.135 | convolution fusion | flops 10066329600 | bytes 26214400 | tf_op jit(solution)/shard_map/td,cdh->tch/dot_general | solution.py:112
  233.6 1.6 copy-done.6
  235.2 21.5 %all-reduce = (f32[640]{0:T(1024)S(1)}, f32[640]{0:T(1024)S(1)}) all-reduce(f32[640]{0:T(1024)S(1)} %get-tuple-element.3, f32[640]{0:T(1024)S(1)} %get-tuple-element.2), channel_id=1, replica_groups=mesh['rep'=4,'tp'=8] {'tp'}, use_global_device_ids=true, to_apply=%region_3.4 | all-reduce | flops 1280 | bytes 10240 | tf_op jit(solution)/shard_map/psum | solution.py:121
  257.9 3.5 %slice.102 = f32[640,4,64]{0,2,1:T(8,128)} slice(f32[640,4,128]{0,2,1:T(8,128)} %multiply_multiply_fusion), slice={[0:640:1], [0:4:1], [0:128:2]} | slice | bytes 1310720 | tf_op jit(solution)/shard_map/slice | solution.py:54
  261.3 1.5 slice.103
  262.9 1.4 slice.165
  264.4 1.5 slice.93
  266.0 1.5 slice.97
  269.4 1.4 maximum_convert_fusion
  283.2 4.2 %all-to-all-start = ((bf16[8,80,512]{2,1,0:T(8,128)(2,1)}), bf16[8,80,512]{2,1,0:T(8,128)(2,1)}, u32[]{:S(2)}, u32[]{:S(2)}) async-start(bf16[8,80,512]{2,1,0:T(8,128)(2,1)} %all_to_all.14), calls=%async_computation | async-start | bytes 1310720 | tf_op jit(solution)/shard_map/all_to_all | solution.py:138
  287.4 5.0 %convert_element_type.94 = bf16[1,40,16,4,128]{2,1,4,3,0:T(8,128)(2,1)} reshape(bf16[640,4,64,2]{0,3,2,1:T(2,128)(2,1)S(1)} %maximum_convert_fusion) | data formatting | bytes 1310720 | tf_op jit(solution)/shard_map/convert_element_type | solution.py:131
  292.7 4.6 %copy.113 = bf16[1,40,16,4,128]{4,2,3,1,0:T(8,128)(2,1)S(1)} copy(bf16[1,40,16,4,128]{2,1,4,3,0:T(8,128)(2,1)} %convert_element_type.94) | data formatting | bytes 1310720 | tf_op jit(solution)/shard_map/convert_element_type | solution.py:131
  299.9 5.6 %scatter_fusion = bf16[2,4,80,16,128]{4,3,2,1,0:T(8,128)(2,1)S(1)} fusion(bf16[2,4,80,16,128]{4,3,2,1,0:T(8,128)(2,1)S(1)} %copy-done.4, s32[40]{0:T(128)S(1)} %compare_select_fusion, bf16[40,2,4,16,128]{4,3,2,1,0:T(8,128)(2,1)} %copy.115), kind=kCustom, calls=%fused_computation | custom fusion | bytes 3932320 | tf_op jit(solution)/shard_map/scatter | solution.py:142
  305.6 2.5 copy.129
  (100 shorter events, 26.2 us)
Async XLA Ops:
  0.6 1.0 copy-start.10
  0.6 1.3 copy-start
  0.6 1.9 copy-start.15
  4.5 21.3 %collective-permute-start = (bf16[1,80,5120]{2,1,0:T(8,128)(2,1)S(1)}, bf16[1,80,5120]{2,1,0:T(8,128)(2,1)S(1)}, u32[]{:S(2)}, u32[]{:S(2)}) collective-permute-start(bf16[1,80,5120]{2,1,0:T(8,128)(2,1)S(1)} %fusion.2), channel_id=1, source_target_pairs={{0,1},{1,0},{2,3},{3,2},{4,5},{5,4},{6,7},{7,6},{8,9},{9,8},{10,11... | collective-permute-start | bytes 2457608 | tf_op jit(solution)/shard_map/ppermute | solution.py:25
  25.9 1.2 copy-start.2
  27.0 37.1 %collective-permute-start.1 = (bf16[2,80,5120]{2,1,0:T(8,128)(2,1)S(1)}, bf16[2,80,5120]{2,1,0:T(8,128)(2,1)}, u32[]{:S(2)}, u32[]{:S(2)}) collective-permute-start(bf16[2,80,5120]{2,1,0:T(8,128)(2,1)S(1)} %pad_maximum_fusion.2), channel_id=1, source_target_pairs={{0,2},{1,3},{2,0},{3,1},{4,6},{5,7},{6,4},{7,5},{8,10},{9,11},{10,... | collective-permute-start | bytes 4915208 | tf_op jit(solution)/shard_map/ppermute | solution.py:25
  66.2 4.6 %copy-start.16 = (s32[3,640]{1,0:T(4,128)S(1)}, s32[3,640]{1,0:T(4,128)}, u32[]{:S(2)}) copy-start(s32[3,640]{1,0:T(4,128)} %param.16) | copy-start | bytes 23044
  66.2 4.7 %copy-start.17 = (f32[2,512]{1,0:T(2,128)S(1)}, f32[2,512]{1,0:T(2,128)}, u32[]{:S(2)}) copy-start(f32[2,512]{1,0:T(2,128)} %param.14) | copy-start | bytes 12292
  66.2 4.7 %copy-start.18 = (f32[64]{0:T(128)S(1)}, f32[64]{0:T(128)}, u32[]{:S(2)}) copy-start(f32[64]{0:T(128)} %constant.47.clone) | copy-start | bytes 772
  66.2 4.7 %copy-start.19 = (f32[64]{0:T(128)S(1)}, f32[64]{0:T(128)}, u32[]{:S(2)}) copy-start(f32[64]{0:T(128)} %constant.48.clone) | copy-start | bytes 772
  66.3 4.7 %copy-start.20 = (f32[64]{0:T(128)S(1)}, f32[64]{0:T(128)}, u32[]{:S(2)}) copy-start(f32[64]{0:T(128)} %constant.49.clone) | copy-start | bytes 772
  68.2 142.6 %collective-permute-start.2 = (bf16[4,80,5120]{2,1,0:T(8,128)(2,1)}, bf16[4,80,5120]{2,1,0:T(8,128)(2,1)}, u32[]{:S(2)}, u32[]{:S(2)}) collective-permute-start(bf16[4,80,5120]{2,1,0:T(8,128)(2,1)} %pad_maximum_fusion.1), channel_id=1, source_target_pairs={{0,4},{1,5},{2,6},{3,7},{4,0},{5,1},{6,2},{7,3},{8,12},{9,13},{10,... | collective-permute-start | bytes 9830408 | tf_op jit(solution)/shard_map/ppermute | solution.py:25
  233.3 1.9 copy-start.6
  257.9 3.5 %copy-start.5 = (f32[640,4,128]{0,2,1:T(8,128)S(1)}, f32[640,4,128]{0,2,1:T(8,128)}, u32[]{:S(2)}) copy-start(f32[640,4,128]{0,2,1:T(8,128)} %multiply_multiply_fusion) | copy-start | bytes 3932164
  264.4 3.1 copy-start.8
  264.4 3.1 copy-start.9
  270.8 1.7 copy-start.7
  274.7 0.9 copy-start.13
  275.6 0.9 copy-start.12
  276.6 0.9 copy-start.11
  282.1 5.3 %copy-start.21 = (s32[40]{0:T(128)S(1)}, s32[40]{0:T(128)}, u32[]{:S(2)}) copy-start(s32[40]{0:T(128)} %param.17) | copy-start | bytes 484
  283.2 22.4 %all-to-all-start = ((bf16[8,80,512]{2,1,0:T(8,128)(2,1)}), bf16[8,80,512]{2,1,0:T(8,128)(2,1)}, u32[]{:S(2)}, u32[]{:S(2)}) async-start(bf16[8,80,512]{2,1,0:T(8,128)(2,1)} %all_to_all.14), calls=%async_computation | async-start | bytes 1310720 | tf_op jit(solution)/shard_map/all_to_all | solution.py:138
  297.7 2.2 copy-start.4
  305.5 2.5 copy-start.3
  (2 other events, 1.8 us)
